TPU v7x, 32 devices: a whole 2x2x4 slice. The times are simulated.
32 devices in a mesh: pix: 4 (over z), mode: 8 (over y, x, core).
Axes of the slice: x: 2, y: 2, z: 4, core: 2. Of those that a mesh axis runs over, the one named last changes fastest.
Arguments:
- frames: float32 [4, 4096, 8192], P(None, 'pix', 'mode'), may hold values from 0 to 500, as said below
- phase_steps: int32 [4], replicated, may hold values from 0 to 3, each once
- pattern_rows: int32 [8192], replicated, may hold values from 0 to 8191, each once
- probes: float32 [2, 32, 8192], replicated, may hold values from -6 to 6
Outputs:
- channels: float32 [2, 32, 8192], replicated
- fields: float32 [2, 32, 4096], P(None, None, ('pix', 'mode'))
- strengths: float32 [32], replicated
Inputs may be any that keep to these rules, and one draw needn't show every extreme that they name: `phase_steps`: each frame has its own phase step. `pattern_rows`: every Hadamard row is displayed exactly once. `frames`: intensities are not negative.
All inputs are finite; a program needn't handle non-finite values.
Results may differ from a plain program's by a relative error of at most 0.0003.
Values sent between devices are 32-bit elements; how exact they have to be, the bound alone decides.
No kernel may reach another device: no remote copies, remote signals or barrier semaphores. Data moves between devices by JAX's collectives and lax.ppermute only.
A program may use at most 128 MiB of HBM per device.

v0:
```python
import math
import jax
import jax.numpy as jnp
from jax import lax
from jax.sharding import PartitionSpec as P

HB = 128
ITERS = 2
precise = lax.Precision.HIGHEST


def demodulate(frames, phase_steps):
    cosine = (phase_steps == 0).astype(jnp.float32) - (phase_steps == 2).astype(jnp.float32)
    sine_part = (phase_steps == 1).astype(jnp.float32) - (phase_steps == 3).astype(jnp.float32)
    real_part = cosine[0] * frames[0]
    imag_part = sine_part[0] * frames[0]
    for frame_index in range(1, frames.shape[0]):
        real_part = real_part + cosine[frame_index] * frames[frame_index]
        imag_part = imag_part + sine_part[frame_index] * frames[frame_index]
    return (0.25 * real_part, 0.25 * imag_part)


def sign_table(table_order):
    positions = jnp.arange(table_order, dtype=jnp.int32)
    common = positions[:, None] & positions[None, :]
    parity = jnp.zeros((table_order, table_order), jnp.int32)
    for bit_place in range(table_order.bit_length() - 1):
        parity = parity + (common >> bit_place & 1)
    return (1 - 2 * (parity & 1)).astype(jnp.float32)


def hadamard_rows(values):
    length = values.shape[-1]
    leading = values.shape[:-1]
    inner_signs = sign_table(HB)
    outer_signs = sign_table(length // HB)
    shaped = values.reshape((-1, length // HB, HB))
    shaped = jnp.matmul(shaped, inner_signs, precision=precise)
    shaped = jnp.einsum("ab,nbc->nac", outer_signs, shaped, precision=precise)
    return shaped.reshape(leading + (length,)) * (1.0 / math.sqrt(length))


def contract_last(first_arg, second_arg):
    return lax.dot_general(first_arg, second_arg, (((1,), (1,)), ((), ())), precision=precise)


def forward(matrix, vectors):
    real_out = contract_last(vectors[0], matrix[0]) - contract_last(vectors[1], matrix[1])
    imag_out = contract_last(vectors[1], matrix[0]) + contract_last(vectors[0], matrix[1])
    return jnp.stack([real_out, imag_out])


def backward(matrix, images):
    real_out = jnp.dot(images[0], matrix[0], precision=precise) + jnp.dot(
        images[1], matrix[1], precision=precise
    )
    imag_out = jnp.dot(images[1], matrix[0], precision=precise) - jnp.dot(
        images[0], matrix[1], precision=precise
    )
    return jnp.stack([real_out, imag_out])


def orthonormal(vectors):
    mode_count = vectors.shape[2]
    stacked = jnp.concatenate([vectors[0], vectors[1]], axis=1)
    gram_matrix = jnp.dot(stacked, stacked.T, precision=precise)
    factor = jnp.linalg.cholesky(gram_matrix)
    solved = lax.linalg.triangular_solve(factor, stacked, left_side=True, lower=True)
    return jnp.stack([solved[:, :mode_count], solved[:, mode_count:]])


def local(frames, phase_steps, pattern_rows, probes):
    columns = frames.shape[2]
    groups = lax.axis_size("mode")
    modes_total = columns * groups
    devices = lax.axis_size("pix") * groups
    real_part, imag_part = demodulate(frames, phase_steps)
    positions = jnp.arange(modes_total, dtype=jnp.int32)
    inverse = jnp.zeros((modes_total,), jnp.int32).at[pattern_rows].set(positions)
    current = orthonormal(probes)
    rows_here = real_part.shape[0] // groups
    demodulated = jnp.stack([real_part, imag_part]).reshape(2, groups, rows_here, columns)
    ordered = jnp.take(
        lax.all_to_all(demodulated, "mode", split_axis=1, concat_axis=3, tiled=True),
        inverse,
        axis=3,
    )
    matrix = hadamard_rows(ordered)
    matrix = matrix.reshape(2, rows_here, modes_total)
    for iteration in range(ITERS):
        images = forward(matrix, current)
        returned = lax.psum(backward(matrix, images), ("pix", "mode"))
        current = orthonormal(returned)
    fields = forward(matrix, current)
    local_power = jnp.sum(fields * fields, axis=(0, 2))
    strengths = lax.psum(local_power, ("pix", "mode")) / (fields.shape[2] * devices)
    channels = math.sqrt(modes_total) * current
    return (channels, fields, strengths)


def solution(mesh):
    in_specs = (P(None, "pix", "mode"), P(), P(), P())
    out_specs = (P(), P(None, None, ("pix", "mode")), P())
    return jax.shard_map(local, mesh=mesh, in_specs=in_specs, out_specs=out_specs, check_vma=False)
```

profile of v0, /device:TPU:0, one launch (start us, length us, event | category | flops | bytes accessed | tf_op | source)
XLA Modules:
  0.0 704.6 jit_solution(8088165573559418275)
XLA Ops:
  7.2 0.7 fusion.188
  7.8 0.7 fusion.211
  8.5 12.0 %add_multiply_fusion.1 = (f32[1,1024,1024]{2,1,0:T(8,128)S(1)}, f32[1,1024,1024]{2,1,0:T(8,128)S(1)}) fusion(f32[4,1024,1024]{2,1,0:T(8,128)} %param.7, f32[]{:T(128)} %bitcast.9, f32[]{:T(128)} %bitcast.8, f32[]{:T(128)} %bitcast.7, f32[]{:T(128)} %bitcast.6, f32[]{:T(128)} %bitcast.14, f32[]{:T(128)} %bitcast.13, f32[]{:T(128)} %bitcast.12, f32[]{:T(128)} %bitcast.11), kind=kLoop, calls=%fused_computation.52 | loop fusion | flops 16777216 | bytes 25165856 | tf_op jit(solution)/shard_map/mul | solution.py:20
  20.5 1.7 pad_maximum_fusion
  22.2 4.1 copy.21
  26.3 5.3 all-to-all-start
  31.8 1.0 copy-done.6
  32.8 1.8 fusion.69
  34.6 2.9 cholesky.59
  37.6 0.6 compare_reduce_fusion.2
  38.2 0.7 fusion.167
  38.9 2.4 custom-call.7
  41.4 30.7 %scatter_custom_fusion = s32[8192]{0:T(1024)S(1)} fusion(s32[8192]{0:T(1024)S(1)} %compare_select_fusion.1, s32[8192]{0:T(1024)S(1)} %iota.46, s32[]{:T(128)} %constant.66.clone.1), kind=kCustom, calls=%fused_computation.208 | custom fusion | bytes 32772 | tf_op jit(solution)/shard_map/scatter | solution.py:79
  72.1 3.1 fusion.68
  75.2 50.9 %all-to-all-done = f32[2,8,128,1024]{3,2,0,1:T(8,128)} async-done(((f32[2,8,128,1024]{3,2,0,1:T(8,128)}), f32[2,8,128,1024]{3,2,0,1:T(8,128)}, u32[]{:S(2)}, u32[]{:S(2)}) %all-to-all-start) | async-done | bytes 8388640 | tf_op jit(solution)/shard_map/all_to_all | solution.py:84
  126.1 8.7 %copy.22 = f32[2,8,128,1024]{2,3,1,0:T(8,128)} copy(f32[2,8,128,1024]{3,2,0,1:T(8,128)} %all-to-all-done) | data formatting | bytes 16777216 | tf_op jit(solution)/shard_map/all_to_all | solution.py:84
  134.8 15.4 %copy.23 = f32[2,128,8192]{1,0,2:T(2,128)} copy(f32[2,128,8192]{1,2,0:T(8,128)} %bitcast.173) | data formatting | bytes 16777216 | tf_op jit(solution)/shard_map/all_to_all | solution.py:84
  150.1 59.4 %gather_fusion = f32[8192,2,128]{2,1,0:T(2,128)} fusion(f32[2,128,8192]{1,0,2:T(2,128)} %copy.23, s32[8192]{0:T(1024)S(1)} %fusion.166), kind=kCustom, calls=%fused_computation | custom fusion | bytes 16809984 | tf_op jit(solution)/shard_map/jit(_take)/gather | solution.py:83
  209.5 11.5 %gather.7 = f32[256,64,128]{0,2,1:T(8,128)} reshape(f32[2,128,8192]{1,0,2:T(2,128)} %bitcast.172) | data formatting | bytes 16777216 | tf_op jit(solution)/shard_map/jit(_take)/gather | solution.py:83
  221.0 8.7 %copy.24 = f32[256,64,128]{2,1,0:T(8,128)} copy(f32[256,64,128]{0,2,1:T(8,128)} %gather.7) | data formatting | bytes 16777216 | tf_op jit(solution)/shard_map/jit(_take)/gather | solution.py:83
  229.7 13.0 %fusion.4 = f32[256,64,128]{2,1,0:T(8,128)S(1)} fusion(f32[256,64,128]{2,1,0:T(8,128)} %copy.24, pred[64,128]{1,0:T(8,128)(4,1)S(1)} %and_bitcast_fusion), kind=kOutput, calls=%fused_computation.12 | convolution fusion | flops 3223732224 | bytes 16785408 | tf_op jit(solution)/shard_map/dot_general | solution.py:38
  242.8 8.9 %multiply_bitcast_fusion = f32[256,64,128]{2,1,0:T(8,128)S(1)} fusion(f32[256,64,128]{2,1,0:T(8,128)S(1)} %fusion.4), kind=kOutput, calls=%fused_computation.11 | convolution fusion | flops 1612800000 | bytes 16777216 | tf_op jit(solution)/shard_map/ab,nbc->nac/dot_general | solution.py:39
  251.6 1.7 fusion.210
  253.3 5.8 fusion.20
  259.1 5.6 fusion.18
  264.7 5.6 fusion.70
  270.3 4.8 fusion.38
  275.0 5.7 fusion.73
  280.7 4.9 fusion.34
  285.6 4.6 fusion.3
  290.2 4.6 fusion.2
  294.8 1.5 pad_maximum_fusion.2
  296.6 134.8 %all-reduce.3.cloned.1.call-done = f32[2,32,8192]{2,1,0:T(8,128)} async-done(((f32[2,32,8192]{2,1,0:T(8,128)}), f32[2,32,8192]{2,1,0:T(8,128)}) %all-reduce.3.cloned.1.call-update) | async-done | bytes 2097168 | tf_op jit(solution)/shard_map/psum | solution.py:92
  431.4 1.7 slice_bitcast_fusion.3
  433.1 1.8 fusion.67
  434.9 2.9 cholesky.70
  437.9 0.6 compare_reduce_fusion.1
  438.5 0.7 fusion.168
  439.2 2.4 custom-call.8
  441.6 1.9 fusion.66
  443.9 5.6 fusion.14
  449.4 5.8 fusion.12
  455.2 5.6 fusion.76
  460.8 4.5 fusion.30
  465.3 6.0 fusion.79
  471.4 4.5 fusion.26
  475.9 4.8 fusion.1
  480.7 4.6 fusion
  485.3 1.5 pad_maximum_fusion.4
  486.8 133.5 %all-reduce.5.cloned.1.call-done = f32[2,32,8192]{2,1,0:T(8,128)} async-done(((f32[2,32,8192]{2,1,0:T(8,128)}), f32[2,32,8192]{2,1,0:T(8,128)}) %all-reduce.5.cloned.1.call-update) | async-done | bytes 2097168 | tf_op jit(solution)/shard_map/psum | solution.py:92
  620.3 1.7 slice_bitcast_fusion.1
  622.0 1.8 fusion.65
  623.8 2.9 cholesky.81
  626.8 0.6 compare_reduce_fusion
  627.4 0.7 fusion.169
  628.1 2.4 custom-call.9
  630.5 1.9 fusion.64
  632.7 5.8 fusion.8
  638.5 5.6 fusion.6
  644.3 5.8 fusion.85
  650.1 5.6 fusion.91
  655.7 0.7 multiply_reduce_fusion
  656.4 38.9 %psum.23 = f32[32]{0:T(128)S(1)} all-reduce(f32[32]{0:T(128)S(1)} %get-tuple-element.5), channel_id=1, replica_groups=mesh['pix'=4,'mode'=8] {'pix','mode'}, use_global_device_ids=true, to_apply=%region_6.9 | all-reduce | flops 32 | bytes 256 | tf_op jit(solution)/shard_map/psum | solution.py:96
  695.9 1.5 maximum_multiply_fusion
  (37 shorter events, 2.1 us)
Async XLA Ops:
  26.3 5.4 copy-start.7
  26.3 99.8 %all-to-all-start = ((f32[2,8,128,1024]{3,2,0,1:T(8,128)}), f32[2,8,128,1024]{3,2,0,1:T(8,128)}, u32[]{:S(2)}, u32[]{:S(2)}) async-start(f32[2,8,128,1024]{3,2,0,1:T(8,128)} %copy.21), calls=%async_computation | async-start | bytes 16777216 | tf_op jit(solution)/shard_map/all_to_all | solution.py:84
  31.6 9.7 %copy-start.8 = (s32[8192]{0:T(1024)S(1)}, s32[8192]{0:T(1024)}, u32[]{:S(2)}) copy-start(s32[8192]{0:T(1024)} %param.9) | copy-start | bytes 98308
  31.6 399.8 %all-reduce.3.cloned.1.call-start = ((), (), s32[]{:S(2)}) async-start(), calls=%async_computation.1 | async-start | bytes 4194304 | tf_op jit(solution)/shard_map/psum | solution.py:92
  31.8 1.0 copy-start.6
  253.3 27.4 %copy-start = (f32[128,64,128]{2,1,0:T(8,128)}, f32[128,64,128]{2,1,0:T(8,128)S(1)}, u32[]{:S(2)}) copy-start(f32[128,64,128]{2,1,0:T(8,128)S(1)} %get-tuple-element.9) | copy-start | bytes 12582916
  253.3 36.9 %copy-start.3 = (f32[128,64,128]{2,1,0:T(8,128)}, f32[128,64,128]{2,1,0:T(8,128)S(1)}, u32[]{:S(2)}) copy-start(f32[128,64,128]{2,1,0:T(8,128)S(1)} %get-tuple-element.10) | copy-start | bytes 12582916
  296.4 323.9 %all-reduce.5.cloned.1.call-start = ((), (), s32[]{:S(2)}) async-start(), calls=%async_computation.2 | async-start | bytes 4194304 | tf_op jit(solution)/shard_map/psum | solution.py:92
  441.6 2.2 copy-start.4
  443.9 11.4 %copy-start.1 = (f32[128,64,128]{2,1,0:T(8,128)S(1)}, f32[128,64,128]{2,1,0:T(8,128)}, u32[]{:S(2)}) copy-start(f32[128,64,128]{2,1,0:T(8,128)} %copy-done) | copy-start | bytes 12582916
  630.5 2.2 copy-start.5
  638.5 5.7 copy-start.2
Sparse Core Ops, SparseCore 0:
  296.5 134.8 all-reduce.2
  486.9 133.3 all-reduce.4
where the time goes:
time: 711 us; the launch traced here: 705 us
  waiting for transfers between devices  319 us (45%)
  local copies, waits for them, and re-layouts  146 us (21%)
  matrix products  140 us (20%)
  other arithmetic  40.2 us (6%)
  blocking collectives  38.9 us (5%)
  between operations  14.9 us (2%)
    psum x2, waiting for transfers between devices, local(): returned = lax.psum(backward(matrix, images), ('pix', 'mode'))  268 us
    gather x3, local copies, waits for them, and re-layouts, local(): jnp.take(lax.all_to_all(demodulated, 'mode', split_axis=1, concat_axis=3,...  79.6 us
    dot_general x12, matrix products, contract_last(): lax.dot_general(first_arg, second_arg, (((1,), (1,)), ((), ())), precisio...  68.3 us
    all_to_all x1, waiting for transfers between devices, local(): lax.all_to_all(demodulated, 'mode', split_axis=1, concat_axis=3, tiled=True)  50.9 us
    psum x1, blocking collectives, local(): lax.psum(local_power, ('pix', 'mode')) / (fields.shape[2] * devices)  38.9 us
    scatter x1, local copies, waits for them, and re-layouts, local(): jnp.zeros((modes_total,), jnp.int32).at[pattern_rows].set(positions)  30.7 us
    all_to_all x2, local copies, waits for them, and re-layouts, local(): lax.all_to_all(demodulated, 'mode', split_axis=1, concat_axis=3, tiled=True)  24 us
  transfers between devices with their start and end apart: 3, of which 3 were waited for; matrix products, arithmetic and copies ran while one was open for 6% of the time, Pallas kernels for 0%

commit v1 on v0

--- a/solution.py
+++ b/solution.py
@@ -93,7 +93,7 @@
         current = orthonormal(returned)
     fields = forward(matrix, current)
     local_power = jnp.sum(fields * fields, axis=(0, 2))
-    strengths = lax.psum(local_power, ("pix", "mode")) / (fields.shape[2] * devices)
+    strengths = lax.psum(lax.psum(local_power, "mode"), "pix") / (fields.shape[2] * devices)
     channels = math.sqrt(modes_total) * current
     return (channels, fields, strengths)
 

time: 711 us -> 694 us (0.976)
  blocking collectives: 38.9 us -> 22.2 us
    psum x1 -> x2, blocking collectives: 38.9 us -> 22.2 us  [the longest x1 11.8 us: local(): lax.psum(local_power, 'mode')]
where the time goes in v1:
time: 694 us; the launch traced here: 688 us
  waiting for transfers between devices  319 us (46%)
  local copies, waits for them, and re-layouts  146 us (21%)
  matrix products  140 us (20%)
  other arithmetic  40.2 us (6%)
  blocking collectives  22.2 us (3%)
  between operations  14.9 us (2%)
    psum x2, waiting for transfers between devices, local(): returned = lax.psum(backward(matrix, images), ('pix', 'mode'))  268 us
    gather x3, local copies, waits for them, and re-layouts, local(): jnp.take(lax.all_to_all(demodulated, 'mode', split_axis=1, concat_axis=3,...  79.6 us
    dot_general x12, matrix products, contract_last(): lax.dot_general(first_arg, second_arg, (((1,), (1,)), ((), ())), precisio...  68.3 us
    all_to_all x1, waiting for transfers between devices, local(): lax.all_to_all(demodulated, 'mode', split_axis=1, concat_axis=3, tiled=True)  50.9 us
    scatter x1, local copies, waits for them, and re-layouts, local(): jnp.zeros((modes_total,), jnp.int32).at[pattern_rows].set(positions)  30.7 us
    all_to_all x2, local copies, waits for them, and re-layouts, local(): lax.all_to_all(demodulated, 'mode', split_axis=1, concat_axis=3, tiled=True)  24 us
  transfers between devices with their start and end apart: 3, of which 3 were waited for; matrix products, arithmetic and copies ran while one was open for 6% of the time, Pallas kernels for 0%

profile of v1, /device:TPU:0, one launch (start us, length us, event | category | flops | bytes accessed | tf_op | source)
XLA Modules:
  0.0 687.9 jit_solution(9773399016544378169)
XLA Ops:
  7.2 0.7 fusion.188
  7.8 0.7 fusion.211
  8.5 12.0 %add_multiply_fusion.1 = (f32[1,1024,1024]{2,1,0:T(8,128)S(1)}, f32[1,1024,1024]{2,1,0:T(8,128)S(1)}) fusion(f32[4,1024,1024]{2,1,0:T(8,128)} %param.7, f32[]{:T(128)} %bitcast.9, f32[]{:T(128)} %bitcast.8, f32[]{:T(128)} %bitcast.7, f32[]{:T(128)} %bitcast.6, f32[]{:T(128)} %bitcast.14, f32[]{:T(128)} %bitcast.13, f32[]{:T(128)} %bitcast.12, f32[]{:T(128)} %bitcast.11), kind=kLoop, calls=%fused_computation.52 | loop fusion | flops 16777216 | bytes 25165856 | tf_op jit(solution)/shard_map/mul | solution.py:20
  20.5 1.7 pad_maximum_fusion
  22.2 4.1 copy.21
  26.3 5.3 all-to-all-start
  31.8 1.0 copy-done.6
  32.8 1.8 fusion.69
  34.6 2.9 cholesky.59
  37.6 0.6 compare_reduce_fusion.2
  38.2 0.7 fusion.167
  38.9 2.4 custom-call.7
  41.4 30.7 %scatter_custom_fusion = s32[8192]{0:T(1024)S(1)} fusion(s32[8192]{0:T(1024)S(1)} %compare_select_fusion.1, s32[8192]{0:T(1024)S(1)} %iota.46, s32[]{:T(128)} %constant.66.clone.1), kind=kCustom, calls=%fused_computation.208 | custom fusion | bytes 32772 | tf_op jit(solution)/shard_map/scatter | solution.py:79
  72.1 3.1 fusion.68
  75.2 50.9 %all-to-all-done = f32[2,8,128,1024]{3,2,0,1:T(8,128)} async-done(((f32[2,8,128,1024]{3,2,0,1:T(8,128)}), f32[2,8,128,1024]{3,2,0,1:T(8,128)}, u32[]{:S(2)}, u32[]{:S(2)}) %all-to-all-start) | async-done | bytes 8388640 | tf_op jit(solution)/shard_map/all_to_all | solution.py:84
  126.1 8.7 %copy.22 = f32[2,8,128,1024]{2,3,1,0:T(8,128)} copy(f32[2,8,128,1024]{3,2,0,1:T(8,128)} %all-to-all-done) | data formatting | bytes 16777216 | tf_op jit(solution)/shard_map/all_to_all | solution.py:84
  134.8 15.4 %copy.23 = f32[2,128,8192]{1,0,2:T(2,128)} copy(f32[2,128,8192]{1,2,0:T(8,128)} %bitcast.173) | data formatting | bytes 16777216 | tf_op jit(solution)/shard_map/all_to_all | solution.py:84
  150.1 59.4 %gather_fusion = f32[8192,2,128]{2,1,0:T(2,128)} fusion(f32[2,128,8192]{1,0,2:T(2,128)} %copy.23, s32[8192]{0:T(1024)S(1)} %fusion.166), kind=kCustom, calls=%fused_computation | custom fusion | bytes 16809984 | tf_op jit(solution)/shard_map/jit(_take)/gather | solution.py:83
  209.5 11.5 %gather.7 = f32[256,64,128]{0,2,1:T(8,128)} reshape(f32[2,128,8192]{1,0,2:T(2,128)} %bitcast.172) | data formatting | bytes 16777216 | tf_op jit(solution)/shard_map/jit(_take)/gather | solution.py:83
  221.0 8.7 %copy.24 = f32[256,64,128]{2,1,0:T(8,128)} copy(f32[256,64,128]{0,2,1:T(8,128)} %gather.7) | data formatting | bytes 16777216 | tf_op jit(solution)/shard_map/jit(_take)/gather | solution.py:83
  229.7 13.0 %fusion.4 = f32[256,64,128]{2,1,0:T(8,128)S(1)} fusion(f32[256,64,128]{2,1,0:T(8,128)} %copy.24, pred[64,128]{1,0:T(8,128)(4,1)S(1)} %and_bitcast_fusion), kind=kOutput, calls=%fused_computation.12 | convolution fusion | flops 3223732224 | bytes 16785408 | tf_op jit(solution)/shard_map/dot_general | solution.py:38
  242.8 8.9 %multiply_bitcast_fusion = f32[256,64,128]{2,1,0:T(8,128)S(1)} fusion(f32[256,64,128]{2,1,0:T(8,128)S(1)} %fusion.4), kind=kOutput, calls=%fused_computation.11 | convolution fusion | flops 1612800000 | bytes 16777216 | tf_op jit(solution)/shard_map/ab,nbc->nac/dot_general | solution.py:39
  251.6 1.7 fusion.210
  253.3 5.8 fusion.20
  259.1 5.6 fusion.18
  264.7 5.6 fusion.70
  270.3 4.8 fusion.38
  275.0 5.7 fusion.73
  280.7 4.9 fusion.34
  285.6 4.6 fusion.3
  290.2 4.6 fusion.2
  294.8 1.5 pad_maximum_fusion.2
  296.6 134.8 %all-reduce.3.cloned.1.call-done = f32[2,32,8192]{2,1,0:T(8,128)} async-done(((f32[2,32,8192]{2,1,0:T(8,128)}), f32[2,32,8192]{2,1,0:T(8,128)}) %all-reduce.3.cloned.1.call-update) | async-done | bytes 2097168 | tf_op jit(solution)/shard_map/psum | solution.py:92
  431.4 1.7 slice_bitcast_fusion.3
  433.1 1.8 fusion.67
  434.9 2.9 cholesky.70
  437.9 0.6 compare_reduce_fusion.1
  438.5 0.7 fusion.168
  439.2 2.4 custom-call.8
  441.6 1.9 fusion.66
  443.9 5.6 fusion.14
  449.4 5.8 fusion.12
  455.2 5.6 fusion.76
  460.8 4.5 fusion.30
  465.3 6.0 fusion.79
  471.4 4.5 fusion.26
  475.9 4.8 fusion.1
  480.7 4.6 fusion
  485.3 1.5 pad_maximum_fusion.4
  486.8 133.5 %all-reduce.5.cloned.1.call-done = f32[2,32,8192]{2,1,0:T(8,128)} async-done(((f32[2,32,8192]{2,1,0:T(8,128)}), f32[2,32,8192]{2,1,0:T(8,128)}) %all-reduce.5.cloned.1.call-update) | async-done | bytes 2097168 | tf_op jit(solution)/shard_map/psum | solution.py:92
  620.3 1.7 slice_bitcast_fusion.1
  622.0 1.8 fusion.65
  623.8 2.9 cholesky.81
  627.4 0.7 fusion.169
  628.1 2.4 custom-call.9
  630.5 1.9 fusion.64
  632.7 5.8 fusion.8
  638.5 5.6 fusion.6
  644.3 5.8 fusion.85
  650.1 5.6 fusion.91
  655.7 0.7 multiply_reduce_fusion
  656.4 11.8 %psum.30 = f32[32]{0:T(128)S(1)} all-reduce(f32[32]{0:T(128)S(1)} %get-tuple-element.5), channel_id=1, replica_groups=mesh['pix'=4,'mode'=8] {'mode'}, use_global_device_ids=true, to_apply=%region_6.9 | all-reduce | flops 32 | bytes 256 | tf_op jit(solution)/shard_map/psum | solution.py:96
  668.2 10.4 %psum.31 = f32[32]{0:T(128)S(1)} all-reduce(f32[32]{0:T(128)S(1)} %psum.30), channel_id=1, replica_groups=mesh['pix'=4,'mode'=8] {'pix'}, use_global_device_ids=true, to_apply=%region_7.10 | all-reduce | flops 32 | bytes 256 | tf_op jit(solution)/shard_map/psum | solution.py:96
  679.1 1.5 maximum_multiply_fusion
  (38 shorter events, 2.7 us)
Async XLA Ops:
  26.3 5.4 copy-start.7
  26.3 99.8 %all-to-all-start = ((f32[2,8,128,1024]{3,2,0,1:T(8,128)}), f32[2,8,128,1024]{3,2,0,1:T(8,128)}, u32[]{:S(2)}, u32[]{:S(2)}) async-start(f32[2,8,128,1024]{3,2,0,1:T(8,128)} %copy.21), calls=%async_computation | async-start | bytes 16777216 | tf_op jit(solution)/shard_map/all_to_all | solution.py:84
  31.6 9.7 %copy-start.8 = (s32[8192]{0:T(1024)S(1)}, s32[8192]{0:T(1024)}, u32[]{:S(2)}) copy-start(s32[8192]{0:T(1024)} %param.9) | copy-start | bytes 98308
  31.6 399.8 %all-reduce.3.cloned.1.call-start = ((), (), s32[]{:S(2)}) async-start(), calls=%async_computation.1 | async-start | bytes 4194304 | tf_op jit(solution)/shard_map/psum | solution.py:92
  31.8 1.0 copy-start.6
  253.3 27.4 %copy-start = (f32[128,64,128]{2,1,0:T(8,128)}, f32[128,64,128]{2,1,0:T(8,128)S(1)}, u32[]{:S(2)}) copy-start(f32[128,64,128]{2,1,0:T(8,128)S(1)} %get-tuple-element.9) | copy-start | bytes 12582916
  253.3 36.9 %copy-start.3 = (f32[128,64,128]{2,1,0:T(8,128)}, f32[128,64,128]{2,1,0:T(8,128)S(1)}, u32[]{:S(2)}) copy-start(f32[128,64,128]{2,1,0:T(8,128)S(1)} %get-tuple-element.10) | copy-start | bytes 12582916
  296.4 323.9 %all-reduce.5.cloned.1.call-start = ((), (), s32[]{:S(2)}) async-start(), calls=%async_computation.2 | async-start | bytes 4194304 | tf_op jit(solution)/shard_map/psum | solution.py:92
  441.6 2.2 copy-start.4
  443.9 11.4 %copy-start.1 = (f32[128,64,128]{2,1,0:T(8,128)S(1)}, f32[128,64,128]{2,1,0:T(8,128)}, u32[]{:S(2)}) copy-start(f32[128,64,128]{2,1,0:T(8,128)} %copy-done) | copy-start | bytes 12582916
  630.5 2.2 copy-start.5
  638.5 5.7 copy-start.2
Sparse Core Ops, SparseCore 0:
  296.5 134.8 all-reduce.2
  486.9 133.3 all-reduce.4
